TPU v7x, 128 devices: a whole 4x4x4 slice. The times are simulated.
128 devices in a mesh: seg: 32 (over x, y, core), cell: 4 (over z).
Axes of the slice: x: 4, y: 4, z: 4, core: 2. Of those that a mesh axis runs over, the one named last changes fastest.
Arguments:
- positions: float32 [512, 3, 512], P(('seg', 'cell')), may hold values from -6 to 6
- rest_shape: float32 [512, 3, 512], P(('seg', 'cell')), may hold values from -6 to 6
- modulus: float32 [512], P(('seg', 'cell')), may hold values from 0.5 to 2
- stiffness: bfloat16 [512, 512], replicated, may hold values from -0.25 to 0.25
- wall_points: float32 [512, 3, 512], P(('seg', 'cell')), may hold values from -6 to 6
- density: float32 [512, 3, 512], P(('seg', 'cell')), may hold values from -6 to 6
- wall_operator: float32 [512, 512], replicated, may hold values from -0.25 to 0.25
- seg_count: int32 [32], P('seg'), may hold values from 1 to 16, as said below
- neighbours: int32 [512, 4], P(('seg', 'cell')), may hold values from 0 to 511, as said below
- near_patches: int32 [512, 2], P(('seg', 'cell')), may hold values from 0 to 511, as said below
Outputs:
- new_positions: float32 [512, 3, 512], P(('seg', 'cell'))
- velocity: float32 [512, 3, 512], P(('seg', 'cell'))
- new_density: float32 [512, 3, 512], P(('seg', 'cell'))
Inputs may be any that keep to these rules, and one draw needn't show every extreme that they name: `seg_count`: live cells of a segment take its slots 0 to count - 1; some segment has 16 live cells and some other has 1. `neighbours`: the first entry of cell c is c itself; every other entry is a live cell of the same segment or of a segment next to it. `near_patches`: every entry is a patch of the cell's own segment or of a segment next to it.
All inputs are finite; a program needn't handle non-finite values.
Results may differ from a plain program's by a relative error of at most 0.0037.
Values sent between devices are 32-bit elements; how exact they have to be, the bound alone decides.
A program may use at most 64 MiB of HBM per device.

v0:
```python
import functools

import jax
import jax.numpy as jnp
from jax import lax
from jax.experimental import pallas as pl
from jax.experimental.pallas import tpu as pltpu
from jax.sharding import PartitionSpec as P

N = 512
OWN = 4
NZ = 4
NB = 4
NW = 2
STEPS = 2
SLOTS = 3 * NZ
PAIRS = OWN * NW
ROWS = 40

soften_square = 0.25
stokes_factor = 0.039788735772973836
relax_factor = 0.5
time_step = 0.5

f32, bf16 = jnp.float32, jnp.bfloat16
MESH = pl.DeviceIdType.MESH


def split3(v):
    a = v.astype(bf16).astype(f32)
    r = v - a
    b = r.astype(bf16).astype(f32)
    return a, b, r - b


def rows8(rows):
    index = lax.broadcasted_iota(jnp.int32, (8, N), 0)
    out = jnp.zeros((8, N), f32)
    for k, row in enumerate(rows):
        out = jnp.where(index == k, jnp.broadcast_to(row, (8, N)), out)
    return out


def dot3(a, b):
    return a[0] * b[0] + a[1] * b[1] + a[2] * b[2]


def source_factor(y):
    p = dot3(y, y)
    a, b, c = split3(rows8([-2.0 * y[0], -2.0 * y[1], -2.0 * y[2], jnp.ones_like(p), p]))
    return jnp.concatenate([a, a, b, a, b, c], 0).astype(bf16)


def target_factor(x):
    q = dot3(x, x) + soften_square
    a, b, c = split3(rows8([x[0], x[1], x[2], q, jnp.ones_like(q)]))
    return jnp.concatenate([a, b, a, c, b, a], 0).astype(bf16)


def moments(y, f):
    p, g = dot3(y, y), dot3(y, f)
    one = rows8([f[0], f[1], f[2], g] + [p * f[k] + g * y[k] for k in range(3)] + [f[0] * y[0]])
    two = rows8([f[l] * y[k] for l in range(3) for k in range(3)][1:])
    a, b, c = split3(jnp.concatenate([one, two], 0))
    return jnp.concatenate([a, b, c], 0).astype(bf16)


def fold(sums):
    return sums[0:16] + sums[16:32] + sums[32:48]


def combine(sums, x):
    row = [sums[k : k + 1] for k in range(16)]
    q = dot3(x, x) + soften_square
    m, g, h = row[0:3], row[3], row[4:7]
    t = [row[7 + 3 * l : 10 + 3 * l] for l in range(3)]
    along = dot3(x, m) - g
    return [
        stokes_factor
        * (
            q * m[k]
            - 2.0 * dot3(x, t[k])
            + h[k]
            + x[k] * along
            - (x[0] * t[0][k] + x[1] * t[1][k] + x[2] * t[2][k])
        )
        for k in range(3)
    ]


def kernel_tile(squares):
    inverse = lax.rsqrt(jnp.maximum(squares, soften_square))
    return (inverse * inverse * inverse).astype(bf16)


def mm(a, b):
    return jnp.dot(a, b, preferred_element_type=f32)


def mt(a, b):
    return lax.dot_general(a, b, (((1,), (1,)), ((), ())), preferred_element_type=f32)


def fused(
    nseg,
    pos_in,
    rest_in,
    modulus,
    stiffness,
    points_in,
    density_in,
    operator,
    seg_count,
    neighbours,
    near,
    pos_out,
    vel_out,
    den_out,
    msg_first,
    msg_second,
    wall,
    xsend,
    xrecv,
    pmat,
    pbuf,
    gcell,
    bcell,
    acc,
    pos,
    rest,
    force,
    den,
    vel,
    pieces,
    onehot,
    op1,
    op2,
    msg_send,
    msg_recv,
    wall_send,
    wall_recv,
    x_send,
    x_recv,
):
    seg = lax.axis_index("seg")
    z = lax.axis_index("cell")
    odd = seg % 2
    partner = seg + 1 - 2 * odd
    across = (seg + 2 * odd - 1 + nseg) % nseg
    own = NZ + z

    def turned(d):
        return (z + d) % NZ

    peers = []
    for step in (0, 1, -1):
        for d in range(NZ):
            if step or d:
                peers.append((step, d))

    barrier = pltpu.get_barrier_semaphore()
    for step, d in peers:
        pl.semaphore_signal(
            barrier, inc=1, device_id=((seg + step + nseg) % nseg, turned(d)), device_id_type=MESH
        )

    for ref in (pos, rest, force, den, vel):
        ref[...] = jnp.zeros_like(ref)
    wall[own] = jnp.zeros((16, N), f32)
    for c in range(OWN):
        for k in range(3):
            r = 3 * c + k
            pos[pl.ds(r, 1), :] = pos_in[c, pl.ds(k, 1), :]
            rest[pl.ds(r, 1), :] = rest_in[c, pl.ds(k, 1), :]
            den[pl.ds(r, 1), :] = density_in[c, pl.ds(k, 1), :]
            wall[own, pl.ds(r, 1), :] = points_in[c, pl.ds(k, 1), :]

    row16 = lax.broadcasted_iota(jnp.int32, (16, N), 0)
    item16 = lax.shift_right_logical(row16 * 43, 7)
    alive = jnp.zeros((16, N), f32)
    scale = jnp.zeros((16, N), f32)
    for c in range(OWN):
        one = jnp.where(z * OWN + c < seg_count[0], 1.0, 0.0).astype(f32)
        alive = jnp.where(item16 == c, one, alive)
        scale = jnp.where(item16 == c, one * modulus[c], scale)

    def send(buffer, source, target, device, send_sem, recv_sem):
        return pltpu.make_async_remote_copy(
            src_ref=buffer.at[source],
            dst_ref=buffer.at[target],
            send_sem=send_sem,
            recv_sem=recv_sem,
            device_id=device,
            device_id_type=MESH,
        )

    def start_own(copy):
        for k, d in enumerate((1, 3, 2)):
            copy(own, own, (seg, turned(d)), k).start()
        copy(own, 8 * odd + z, (partner, z), 3).start()
        copy(own, 8 - 8 * odd + z, (across, z), 4).start()

    def hand_on(copy, which):
        for k, d in which:
            slot = NZ + turned(d)
            copy(slot, slot, (seg, turned(d)), 0).wait_recv()
            copy(slot, 8 - 8 * odd + turned(d), (across, z), 5 + 2 * k).start()
            copy(slot, 8 * odd + turned(d), (partner, z), 6 + 2 * k).start()

    def wait_sides(copy):
        for d in range(NZ):
            for base in (0, 8):
                slot = base + turned(d)
                copy(slot, slot, (partner, z), 0).wait_recv()

    def wait_sent(copy):
        for k in range(11):
            copy(own, own, (partner, z), k).wait_send()

    def wall_copy(source, target, device, k):
        return send(wall, source, target, device, wall_send.at[k], wall_recv.at[target])

    first = (seg - 1) * OWN * NZ

    pl.semaphore_wait(barrier, len(peers))
    start_own(wall_copy)

    def cut(i, _):
        at = pl.ds(pl.multiple_of(i * 64, 64), 64)
        whole = operator[at, :]
        high = whole.astype(bf16)
        op1[at, :] = high
        op2[at, :] = (whole - high.astype(f32)).astype(bf16)
        return 0

    lax.fori_loop(0, N // 64, cut, 0)

    hot_row = lax.broadcasted_iota(jnp.int32, (16, 128), 0)
    hot_col = lax.broadcasted_iota(jnp.int32, (16, 128), 1)
    row_item = lax.shift_right_logical(hot_row * 43, 7)
    row_part = hot_row - 3 * row_item
    col = hot_col - jnp.where(hot_col >= 24, 24, 0) - jnp.where(hot_col >= 48, 24, 0)
    col_pair = lax.shift_right_logical(col * 43, 7)
    col_part = col - 3 * col_pair
    wanted = jnp.full((16, 128), -1, jnp.int32)
    for c in range(OWN):
        for w in range(NW):
            wanted = jnp.where(col_pair == c * NW + w, near[c, w] - first, wanted)
    fits = (row_part == col_part) & (row_item < OWN) & (hot_col < 72)
    for g in range(SLOTS):
        hit = fits & (row_item + g * OWN == wanted)
        onehot[pl.ds(g * 16, 16), :] = jnp.where(hit, 1.0, 0.0).astype(bf16)

    def rows_of(ref, base):
        return [ref[pl.ds(base + k, 1), :] for k in range(3)]

    def tiles(source, target, store):
        for k in range(4):
            store(k, kernel_tile(mm(source[k * 128 : (k + 1) * 128], target)))

    def near_rows(c, w):
        relative = jnp.clip(near[c, w] - first, 0, SLOTS * OWN - 1)
        slot, item = lax.shift_right_logical(relative, 2), lax.bitwise_and(relative, 3)
        return slot, 3 * item

    def one_step(step, msg):
        def msg_copy(source, target, device, k):
            return send(
                msg, source, target, device, msg_send.at[step, k], msg_recv.at[step, target]
            )

        offset = (pos[...] - rest[...]).astype(bf16)
        force[...] = mt(offset, stiffness[...]) * scale
        msg[own, 0:12, :] = pos[0:12, :]
        msg[own, 12:24, :] = force[0:12, :]
        msg[own, 24:36, :] = den[0:12, :]
        msg[own, 36:40, :] = jnp.zeros((4, N), f32)
        start_own(msg_copy)

        for c in range(OWN):
            x, f = rows_of(pos, 3 * c), rows_of(force, 3 * c)
            g, b = moments(x, f), target_factor(x)
            gcell[c] = g
            bcell[c] = b
            slot = c % 2

            def keep(k, value):
                pbuf[slot, pl.ds(k * 128, 128), :] = value

            tiles(source_factor(x).T, b, keep)
            acc[c] = fold(mm(g, pbuf[slot]))

        if step == 0:
            hand_on(wall_copy, ((0, 1), (1, 3), (2, 2)))
            wait_sides(wall_copy)

        hand_on(msg_copy, ((0, 1), (1, 3)))

        def reverse(c, _):
            for w in range(NW):
                slot, base = near_rows(c, w)
                y = [wall[slot, pl.ds(base + k, 1), :] for k in range(3)]
                pair = c * NW + w

                def keep(k, value):
                    pmat[pair, pl.ds(k * 128, 128), :] = value

                tiles(source_factor(y).T, bcell[c], keep)
                out = combine(fold(mt(gcell[c], pmat[pair])), y)
                for k in range(3):
                    pieces[pl.ds(3 * pair + k, 1), :] = out[k]
            return 0

        lax.fori_loop(0, OWN, reverse, 0)
        hand_on(msg_copy, ((2, 2),))

        high, middle, low = split3(pieces[...])
        spread = jnp.concatenate([high, middle, low, jnp.zeros((56, N), f32)], 0).astype(bf16)
        shares = mm(onehot[...], spread)
        for g in range(SLOTS):
            xsend[step, g] = shares[g * 16 : (g + 1) * 16]

        def x_copy(group, target, device, k):
            return pltpu.make_async_remote_copy(
                src_ref=xsend.at[step, group],
                dst_ref=xrecv.at[step, target],
                send_sem=x_send.at[step, k],
                recv_sem=x_recv.at[step, target],
                device_id=device,
                device_id_type=MESH,
            )

        for k, (away, d) in enumerate(peers):
            x_copy(
                (away + 1) * NZ + turned(d),
                (1 - away) * NZ + z,
                ((seg + away + nseg) % nseg, turned(d)),
                k,
            ).start()

        high, middle, low = split3(den[...])
        layered = fold(mt(jnp.concatenate([high, middle, low], 0).astype(bf16), op1[...]))
        second = mt(jnp.concatenate([high, middle], 0).astype(bf16), op2[...])
        layered = layered + second[0:16] + second[16:32]

        wait_sides(msg_copy)

        def forward(c, _):
            total = acc[c]
            sums = None
            for w in range(NW):
                slot, base = near_rows(c, w)
                y = [wall[slot, pl.ds(base + k, 1), :] for k in range(3)]
                f = [msg[slot, pl.ds(24 + base + k, 1), :] for k in range(3)]
                part = mm(moments(y, f), pmat[c * NW + w])
                sums = part if sums is None else sums + part
            b = bcell[c]
            for n in range(1, NB):
                relative = jnp.clip(neighbours[c, n] - first, 0, SLOTS * OWN - 1)
                slot = lax.shift_right_logical(relative, 2)
                base = 3 * lax.bitwise_and(relative, 3)
                y = [msg[slot, pl.ds(base + k, 1), :] for k in range(3)]
                f = [msg[slot, pl.ds(12 + base + k, 1), :] for k in range(3)]

                def keep(k, value):
                    pbuf[n % 2, pl.ds(k * 128, 128), :] = value

                tiles(source_factor(y).T, b, keep)
                sums = sums + mm(moments(y, f), pbuf[n % 2])
            total = total + fold(sums)
            x = rows_of(pos, 3 * c)
            out = combine(total, x)
            for k in range(3):
                vel[pl.ds(3 * c + k, 1), :] = out[k]
            return 0

        lax.fori_loop(0, OWN, forward, 0)
        speed = alive * vel[...]
        vel[...] = speed
        pos[...] = pos[...] + time_step * speed

        flow = xsend[step, own]
        for k, (away, d) in enumerate(peers):
            slot = (1 + away) * NZ + turned(d)
            x_copy(own, slot, (seg, turned(d)), k).wait_recv()
            flow = flow + xrecv[step, slot]
        old = den[...]
        den[...] = old - relax_factor * (flow + 0.5 * old + layered)

        wait_sent(msg_copy)
        for k in range(11):
            x_copy(own, own, (partner, z), k).wait_send()

    for step, msg in enumerate((msg_first, msg_second)):
        one_step(step, msg)
    wait_sent(wall_copy)

    for c in range(OWN):
        for k in range(3):
            r = 3 * c + k
            pos_out[c, pl.ds(k, 1), :] = pos[pl.ds(r, 1), :]
            vel_out[c, pl.ds(k, 1), :] = vel[pl.ds(r, 1), :]
            den_out[c, pl.ds(k, 1), :] = den[pl.ds(r, 1), :]


def body(
    positions,
    rest_shape,
    modulus,
    stiffness,
    wall_points,
    density,
    wall_operator,
    seg_count,
    neighbours,
    near_patches,
):
    nseg = lax.axis_size("seg")
    vmem = pl.BlockSpec(memory_space=pltpu.VMEM)
    smem = pl.BlockSpec(memory_space=pltpu.SMEM)
    shape = jax.ShapeDtypeStruct((OWN, 3, N), f32)
    dma = pltpu.SemaphoreType.DMA
    return pl.pallas_call(
        functools.partial(fused, nseg),
        out_shape=(shape, shape, shape),
        in_specs=[vmem, vmem, smem, vmem, vmem, vmem, vmem, smem, smem, smem],
        out_specs=(vmem, vmem, vmem),
        scratch_shapes=[
            pltpu.VMEM((SLOTS, ROWS, N), f32),
            pltpu.VMEM((SLOTS, ROWS, N), f32),
            pltpu.VMEM((SLOTS, 16, N), f32),
            pltpu.VMEM((STEPS, SLOTS, 16, N), f32),
            pltpu.VMEM((STEPS, SLOTS, 16, N), f32),
            pltpu.VMEM((PAIRS, N, N), bf16),
            pltpu.VMEM((2, N, N), bf16),
            pltpu.VMEM((OWN, 48, N), bf16),
            pltpu.VMEM((OWN, 48, N), bf16),
            pltpu.VMEM((OWN, 16, N), f32),
            pltpu.VMEM((16, N), f32),
            pltpu.VMEM((16, N), f32),
            pltpu.VMEM((16, N), f32),
            pltpu.VMEM((16, N), f32),
            pltpu.VMEM((16, N), f32),
            pltpu.VMEM((3 * PAIRS, N), f32),
            pltpu.VMEM((SLOTS * 16, 128), bf16),
            pltpu.VMEM((N, N), bf16),
            pltpu.VMEM((N, N), bf16),
            dma((STEPS, 11)),
            dma((STEPS, SLOTS)),
            dma((11,)),
            dma((SLOTS,)),
            dma((STEPS, 11)),
            dma((STEPS, SLOTS)),
        ],
        compiler_params=pltpu.CompilerParams(collective_id=0, has_side_effects=True),
        name="red_cell_steps",
    )(
        positions,
        rest_shape,
        modulus,
        stiffness,
        wall_points,
        density,
        wall_operator,
        seg_count,
        neighbours,
        near_patches,
    )


def solution(mesh):
    placed = (
        P(("seg", "cell"), None, None),
        P(("seg", "cell"), None, None),
        P(("seg", "cell")),
        P(),
        P(("seg", "cell"), None, None),
        P(("seg", "cell"), None, None),
        P(),
        P("seg"),
        P(("seg", "cell"), None),
        P(("seg", "cell"), None),
    )
    return jax.shard_map(
        body,
        mesh=mesh,
        in_specs=placed,
        out_specs=(
            P(("seg", "cell"), None, None),
            P(("seg", "cell"), None, None),
            P(("seg", "cell"), None, None),
        ),
        check_vma=False,
    )
```

profile of v0, /device:TPU:31, one launch (start us, length us, event | category | flops | bytes accessed | tf_op | source)
XLA Modules:
  0.0 60.2 jit_solution(13514269548608505356)
XLA Ops:
  0.6 0.0 copy-start.5
  1.3 0.0 copy-done.5
  1.3 0.7 %copy.17.near = s32[4,2]{1,0:T(4,128)} copy(s32[4,2]{0,1:T(2,128)S(1)} %copy-done.5) | data formatting | bytes 64 | tf_op args[9]
  2.0 0.0 copy-start.2
  2.0 1.4 %copy.13.pos_in = f32[4,3,512]{2,1,0:T(4,128)} copy(f32[4,3,512]{2,0,1:T(4,128)} %param.10) | data formatting | bytes 49152 | tf_op args[0]
  3.3 0.0 copy-done.2
  3.3 0.0 copy-start.3
  3.3 0.6 %copy.14.rest_in = f32[4,3,512]{2,1,0:T(4,128)} copy(f32[4,3,512]{2,0,1:T(4,128)S(1)} %copy-done.2) | data formatting | bytes 49152 | tf_op args[1]
  4.0 0.1 copy-done.3
  4.1 0.0 copy-start.4
  4.1 0.6 %copy.15.points_in = f32[4,3,512]{2,1,0:T(4,128)} copy(f32[4,3,512]{2,0,1:T(4,128)S(1)} %copy-done.3) | data formatting | bytes 49152 | tf_op args[4]
  4.7 0.1 copy-done.4
  4.8 0.6 %copy.16.density_in = f32[4,3,512]{2,1,0:T(4,128)} copy(f32[4,3,512]{2,0,1:T(4,128)S(1)} %copy-done.4) | data formatting | bytes 49152 | tf_op args[5]
  5.5 52.0 %red_cell_steps.1 = (f32[4,3,512]{2,1,0:T(4,128)}, f32[4,3,512]{2,1,0:T(4,128)}, f32[4,3,512]{2,1,0:T(4,128)}) custom-call(f32[4,3,512]{2,1,0:T(4,128)} %copy.13.pos_in, f32[4,3,512]{2,1,0:T(4,128)} %copy.14.rest_in, f32[4]{0:T(128)} %modulus.1, bf16[512,512]{1,0:T(8,128)(2,1)} %stiffness.1, f32[4,3,512]{2,1,0:T(4,128)} %copy.15.points_in, ...), custom_call_target="tpu_custom_call" | custom-call | tf_op jit(solution)/shard_map/red_cell_steps/pallas_call | solution.py:423
  57.5 0.0 copy-start.1
  57.5 1.4 %copy.18 = f32[4,3,512]{2,0,1:T(4,128)} copy(f32[4,3,512]{2,1,0:T(4,128)} %get-tuple-element.3) | data formatting | bytes 49152 | tf_op jit(solution)/shard_map/red_cell_steps/pallas_call | solution.py:423
  58.9 0.0 copy-done.1
  58.9 0.0 copy-start
  58.9 0.6 %copy.19 = f32[4,3,512]{2,0,1:T(4,128)} copy(f32[4,3,512]{2,1,0:T(4,128)S(1)} %copy-done.1) | data formatting | bytes 49152 | tf_op jit(solution)/shard_map/red_cell_steps/pallas_call | solution.py:423
  59.5 0.1 copy-done
  59.6 0.6 %copy.20 = f32[4,3,512]{2,0,1:T(4,128)} copy(f32[4,3,512]{2,1,0:T(4,128)S(1)} %copy-done) | data formatting | bytes 49152 | tf_op jit(solution)/shard_map/red_cell_steps/pallas_call | solution.py:423
Async XLA Ops:
  0.6 0.7 %copy-start.5 = (s32[4,2]{0,1:T(2,128)S(1)}, s32[4,2]{0,1:T(2,128)}, u32[]{:S(2)}) copy-start(s32[4,2]{0,1:T(2,128)} %param.19) | copy-start | bytes 100
  2.0 1.4 %copy-start.2 = (f32[4,3,512]{2,0,1:T(4,128)S(1)}, f32[4,3,512]{2,0,1:T(4,128)}, u32[]{:S(2)}) copy-start(f32[4,3,512]{2,0,1:T(4,128)} %param.11) | copy-start | bytes 73732
  3.3 0.7 %copy-start.3 = (f32[4,3,512]{2,0,1:T(4,128)S(1)}, f32[4,3,512]{2,0,1:T(4,128)}, u32[]{:S(2)}) copy-start(f32[4,3,512]{2,0,1:T(4,128)} %param.14) | copy-start | bytes 73732
  4.1 0.7 %copy-start.4 = (f32[4,3,512]{2,0,1:T(4,128)S(1)}, f32[4,3,512]{2,0,1:T(4,128)}, u32[]{:S(2)}) copy-start(f32[4,3,512]{2,0,1:T(4,128)} %param.15) | copy-start | bytes 73732
  57.5 1.4 %copy-start.1 = (f32[4,3,512]{2,1,0:T(4,128)S(1)}, f32[4,3,512]{2,1,0:T(4,128)}, u32[]{:S(2)}) copy-start(f32[4,3,512]{2,1,0:T(4,128)} %get-tuple-element.4) | copy-start | bytes 73732
  58.9 0.8 %copy-start = (f32[4,3,512]{2,1,0:T(4,128)S(1)}, f32[4,3,512]{2,1,0:T(4,128)}, u32[]{:S(2)}) copy-start(f32[4,3,512]{2,1,0:T(4,128)} %get-tuple-element.5) | copy-start | bytes 73732
where the time goes:
time: 60.7 us; the launch traced here: 60.2 us
  Pallas kernels  52 us (86%)
  local copies, waits for them, and re-layouts  6.91 us (11%)
  between operations  1.32 us (2%)
    pallas_call x1, Pallas kernels, body(): pl.pallas_call(functools.partial(fused, nseg), out_shape=(shape, shape, s...  52 us
    unnamed x17, local copies, waits for them, and re-layouts  4.29 us
    pallas_call x3, local copies, waits for them, and re-layouts, body(): pl.pallas_call(functools.partial(fused, nseg), out_shape=(shape, shape, s...  2.62 us

commit v1 on v0

v1 whole, which is shorter than its diff:
```python
import functools

import jax
import jax.numpy as jnp
from jax import lax
from jax.experimental import pallas as pl
from jax.experimental.pallas import tpu as pltpu
from jax.sharding import PartitionSpec as P

N = 512
OWN = 4
NZ = 4
NB = 4
NW = 2
STEPS = 2
SLOTS = 3 * NZ
PAIRS = OWN * NW

soften_square = 0.25
stokes_factor = 0.039788735772973836
relax_factor = 0.5
time_step = 0.5

f32, bf16 = jnp.float32, jnp.bfloat16
MESH = pl.DeviceIdType.MESH


def split3(v):
    a = v.astype(bf16).astype(f32)
    r = v - a
    b = r.astype(bf16).astype(f32)
    return a, b, r - b


def rows8(rows):
    index = lax.broadcasted_iota(jnp.int32, (8, N), 0)
    out = jnp.zeros((8, N), f32)
    for k, row in enumerate(rows):
        out = jnp.where(index == k, jnp.broadcast_to(row, (8, N)), out)
    return out


def dot3(a, b):
    return a[0] * b[0] + a[1] * b[1] + a[2] * b[2]


def source_factor(y):
    p = dot3(y, y)
    a, b, c = split3(rows8([-2.0 * y[0], -2.0 * y[1], -2.0 * y[2], jnp.ones_like(p), p]))
    return jnp.concatenate([a, a, b, a, b, c], 0).astype(bf16)


def target_factor(x):
    q = dot3(x, x) + soften_square
    a, b, c = split3(rows8([x[0], x[1], x[2], q, jnp.ones_like(q)]))
    return jnp.concatenate([a, b, a, c, b, a], 0).astype(bf16)


def moments(y, f):
    p, g = dot3(y, y), dot3(y, f)
    one = rows8([f[0], f[1], f[2], g] + [p * f[k] + g * y[k] for k in range(3)] + [f[0] * y[0]])
    two = rows8([f[l] * y[k] for l in range(3) for k in range(3)][1:])
    a, b, c = split3(jnp.concatenate([one, two], 0))
    return jnp.concatenate([a, b, c], 0).astype(bf16)


def fold(sums):
    return sums[0:16] + sums[16:32] + sums[32:48]


def combine(sums, x):
    row = [sums[k : k + 1] for k in range(16)]
    q = dot3(x, x) + soften_square
    m, g, h = row[0:3], row[3], row[4:7]
    t = [row[7 + 3 * l : 10 + 3 * l] for l in range(3)]
    along = dot3(x, m) - g
    return [
        stokes_factor
        * (
            q * m[k]
            - 2.0 * dot3(x, t[k])
            + h[k]
            + x[k] * along
            - (x[0] * t[0][k] + x[1] * t[1][k] + x[2] * t[2][k])
        )
        for k in range(3)
    ]


def kernel_tile(squares):
    inverse = lax.rsqrt(jnp.maximum(squares, soften_square))
    return (inverse * inverse * inverse).astype(bf16)


def mm(a, b):
    return jnp.dot(a, b, preferred_element_type=f32)


def mt(a, b):
    return lax.dot_general(a, b, (((1,), (1,)), ((), ())), preferred_element_type=f32)


def fused(
    nseg,
    pos_in,
    rest_in,
    modulus,
    stiffness,
    points_in,
    density_in,
    operator,
    seg_count,
    neighbours,
    near,
    pos_out,
    vel_out,
    den_out,
    wall,
    cells_first,
    cells_second,
    den_first,
    den_second,
    xsend,
    xrecv,
    pmat,
    pbuf,
    gcell,
    bcell,
    acc,
    pos,
    rest,
    force,
    den,
    vel,
    pieces,
    onehot,
    op1,
    op2,
    send_sem,
    recv_sem,
    x_send,
    x_recv,
):
    seg = lax.axis_index("seg")
    z = lax.axis_index("cell")
    odd = seg % 2
    partner = seg + 1 - 2 * odd
    across = (seg + 2 * odd - 1 + nseg) % nseg
    own = NZ + z

    def turned(d):
        return (z + d) % NZ

    peers = []
    for away in (0, 1, -1):
        for d in range(NZ):
            if away or d:
                peers.append((away, d))

    barrier = pltpu.get_barrier_semaphore()
    for away, d in peers:
        pl.semaphore_signal(
            barrier, inc=1, device_id=((seg + away + nseg) % nseg, turned(d)), device_id_type=MESH
        )

    for ref in (pos, rest, force, den, vel):
        ref[...] = jnp.zeros_like(ref)
    for k in range(3):
        at = pl.ds(4 * k, 4)
        pos[at, :] = pos_in[k]
        rest[at, :] = rest_in[k]
        den[at, :] = density_in[k]
        wall[own, at, :] = points_in[k]

    item16 = lax.bitwise_and(lax.broadcasted_iota(jnp.int32, (16, N), 0), 3)
    alive = jnp.zeros((16, N), f32)
    scale = jnp.zeros((16, N), f32)
    for c in range(OWN):
        one = jnp.where(z * OWN + c < seg_count[0], 1.0, 0.0).astype(f32)
        alive = jnp.where(item16 == c, one, alive)
        scale = jnp.where(item16 == c, one * modulus[c], scale)

    class Message:
        def __init__(self, buffer, number):
            self.buffer, self.number = buffer, number

        def copy(self, source, target, device, k):
            return pltpu.make_async_remote_copy(
                src_ref=self.buffer.at[source],
                dst_ref=self.buffer.at[target],
                send_sem=send_sem.at[self.number, k],
                recv_sem=recv_sem.at[self.number, target],
                device_id=device,
                device_id_type=MESH,
            )

        def start(self):
            for k, d in enumerate((1, 3, 2)):
                self.copy(own, own, (seg, turned(d)), k).start()
            self.copy(own, 8 - 8 * odd + z, (across, z), 4).start()
            self.copy(own, 8 * odd + z, (partner, z), 3).start()

        def relay(self, *which):
            for d in which:
                slot = NZ + turned(d)
                self.copy(slot, slot, (seg, turned(d)), 0).wait_recv()
                self.copy(slot, 8 - 8 * odd + turned(d), (across, z), 3 + 2 * d).start()
                self.copy(slot, 8 * odd + turned(d), (partner, z), 4 + 2 * d).start()

        def arrived(self):
            for d in range(NZ):
                for base in (0, 8):
                    slot = base + turned(d)
                    self.copy(slot, slot, (partner, z), 0).wait_recv()

        def sent(self):
            for k in range(11):
                self.copy(own, own, (partner, z), k).wait_send()

    walls = Message(wall, 0)
    cell_messages = [Message(cells_first, 1), Message(cells_second, 2)]
    den_messages = [Message(den_first, 3), Message(den_second, 4)]
    first = (seg - 1) * OWN * NZ

    def rows_of(ref, item):
        return [ref[pl.ds(4 * k + item, 1), :] for k in range(3)]

    def rows_at(ref, slot, item, base=0):
        return [ref[slot, pl.ds(base + 4 * k + item, 1), :] for k in range(3)]

    def place(number):
        relative = jnp.clip(number - first, 0, SLOTS * OWN - 1)
        return lax.shift_right_logical(relative, 2), lax.bitwise_and(relative, 3)

    def tiles(source, target, ref, index):
        for k in range(4):
            ref[index, pl.ds(k * 128, 128), :] = kernel_tile(
                mm(source[k * 128 : (k + 1) * 128], target)
            )

    def make_forces():
        offset = (pos[...] - rest[...]).astype(bf16)
        force[...] = mt(offset, stiffness[...]) * scale

    def pack(step):
        buffer = cell_messages[step].buffer
        buffer[own, 0:12, :] = pos[0:12, :]
        buffer[own, 12:24, :] = force[0:12, :]
        den_messages[step].buffer[own] = den[0:12, :]

    def itself():
        for c in range(OWN):
            x, f = rows_of(pos, c), rows_of(force, c)
            g, b = moments(x, f), target_factor(x)
            gcell[c] = g
            bcell[c] = b
            tiles(source_factor(x).T, b, pbuf, c)
            acc[c] = fold(mm(g, pbuf[c]))

    def by_halves(work, between):
        def trip(h, _):
            work(2 * h)

            @pl.when(h == 0)
            def _():
                between()

            return 0

        lax.fori_loop(0, 2, trip, 0)

    def reverse(cell):
        for i in range(2):
            for w in range(NW):
                c = cell + i
                slot, item = place(near[w, c])
                y = rows_at(wall, slot, item)
                pair = c * NW + w
                tiles(source_factor(y).T, bcell[c], pmat, pair)
                out = combine(fold(mt(gcell[c], pmat[pair])), y)
                for k in range(3):
                    pieces[pl.ds(3 * pair + k, 1), :] = out[k]

    def listed(step, cell):
        ref = cell_messages[step].buffer
        for i in range(2):
            c = cell + i
            b = bcell[c]
            sums = None
            for n in range(1, NB):
                slot, item = place(neighbours[c, n])
                y, f = rows_at(ref, slot, item), rows_at(ref, slot, item, 12)
                buffer = i * 3 + n - 1
                tiles(source_factor(y).T, b, pbuf, buffer)
                part = mm(moments(y, f), pbuf[buffer])
                sums = part if sums is None else sums + part
            acc[c] = acc[c] + fold(sums)

    def from_walls(step, cell):
        for i in range(2):
            c = cell + i
            sums = None
            for w in range(NW):
                slot, item = place(near[w, c])
                y, f = rows_at(wall, slot, item), rows_at(den_messages[step].buffer, slot, item)
                part = mm(moments(y, f), pmat[c * NW + w])
                sums = part if sums is None else sums + part
            out = combine(acc[c] + fold(sums), rows_of(pos, c))
            for k in range(3):
                vel[pl.ds(4 * k + c, 1), :] = out[k]

    def x_copy(step, group, target, device, k):
        return pltpu.make_async_remote_copy(
            src_ref=xsend.at[step, group],
            dst_ref=xrecv.at[step, target],
            send_sem=x_send.at[step, k],
            recv_sem=x_recv.at[step, target],
            device_id=device,
            device_id_type=MESH,
        )

    def send_pieces(step):
        high, middle, low = split3(pieces[...])
        spread = jnp.concatenate([high, middle, low, jnp.zeros((56, N), f32)], 0).astype(bf16)
        shares = mm(onehot[...], spread)
        for g in range(SLOTS):
            xsend[step, g] = shares[g * 16 : g * 16 + 12]
        for k, (away, d) in enumerate(peers):
            x_copy(
                step,
                (away + 1) * NZ + turned(d),
                (1 - away) * NZ + z,
                ((seg + away + nseg) % nseg, turned(d)),
                k,
            ).start()

    def operate():
        high, middle, low = split3(den[...])
        layered = fold(mt(jnp.concatenate([high, middle, low], 0).astype(bf16), op1[...]))
        second = mt(jnp.concatenate([high, middle], 0).astype(bf16), op2[...])
        return layered + second[0:16] + second[16:32]

    def move():
        speed = alive * vel[...]
        vel[...] = speed
        pos[...] = pos[...] + time_step * speed

    def update_density(step, layered):
        flow = xsend[step, own]
        for k, (away, d) in enumerate(peers):
            slot = (1 + away) * NZ + turned(d)
            x_copy(step, own, slot, (seg, turned(d)), k).wait_recv()
            flow = flow + xrecv[step, slot]
        old = den[0:12, :]
        den[0:12, :] = old - relax_factor * (flow + 0.5 * old + layered[0:12])

    def cut(i, _):
        at = pl.ds(pl.multiple_of(i * 64, 64), 64)
        whole = operator[at, :]
        high = whole.astype(bf16)
        op1[at, :] = high
        op2[at, :] = (whole - high.astype(f32)).astype(bf16)
        return 0

    def choose():
        hot_row = lax.broadcasted_iota(jnp.int32, (16, 128), 0)
        hot_col = lax.broadcasted_iota(jnp.int32, (16, 128), 1)
        row_item, row_part = lax.bitwise_and(hot_row, 3), lax.shift_right_logical(hot_row, 2)
        col = hot_col - jnp.where(hot_col >= 24, 24, 0) - jnp.where(hot_col >= 48, 24, 0)
        col_pair = lax.shift_right_logical(col * 43, 7)
        col_part = col - 3 * col_pair
        wanted = jnp.full((16, 128), -1, jnp.int32)
        for c in range(OWN):
            for w in range(NW):
                wanted = jnp.where(col_pair == c * NW + w, near[w, c] - first, wanted)
        fits = (row_part == col_part) & (hot_col < 72)
        for g in range(SLOTS):
            hit = fits & (row_item + g * OWN == wanted)
            onehot[pl.ds(g * 16, 16), :] = jnp.where(hit, 1.0, 0.0).astype(bf16)

    make_forces()
    pack(0)
    choose()
    lax.fori_loop(0, N // 64, cut, 0)

    pl.semaphore_wait(barrier, len(peers))
    walls.start()
    cell_messages[0].start()
    itself()
    walls.relay(1, 3, 2)
    den_messages[0].start()
    walls.arrived()
    cell_messages[0].relay(1, 3)

    for step in range(STEPS):
        cells, dens = cell_messages[step], den_messages[step]
        if step == 1:
            make_forces()
            pack(step)
            cells.start()
            dens.start()
            itself()
            by_halves(reverse, lambda: cells.relay(1, 3))
        else:
            by_halves(reverse, lambda: cells.relay(2))
        if step == 1:
            cells.relay(2)
        send_pieces(step)
        dens.relay(1, 3)
        layered = operate()
        dens.relay(2)
        cells.arrived()
        by_halves(functools.partial(listed, step), lambda: None)
        dens.arrived()
        by_halves(functools.partial(from_walls, step), lambda: None)
        move()
        update_density(step, layered)

    walls.sent()
    for step in range(STEPS):
        cell_messages[step].sent()
        den_messages[step].sent()
        for k in range(11):
            x_copy(step, own, own, (partner, z), k).wait_send()

    for k in range(3):
        at = pl.ds(4 * k, 4)
        pos_out[k] = pos[at, :]
        vel_out[k] = vel[at, :]
        den_out[k] = den[at, :]


def body(
    positions,
    rest_shape,
    modulus,
    stiffness,
    wall_points,
    density,
    wall_operator,
    seg_count,
    neighbours,
    near_patches,
):
    nseg = lax.axis_size("seg")
    vmem = pl.BlockSpec(memory_space=pltpu.VMEM)
    smem = pl.BlockSpec(memory_space=pltpu.SMEM)
    shape = jax.ShapeDtypeStruct((3, OWN, N), f32)
    dma = pltpu.SemaphoreType.DMA

    def turn(array):
        return jnp.transpose(array, (1, 0, 2))

    outs = pl.pallas_call(
        functools.partial(fused, nseg),
        out_shape=(shape, shape, shape),
        in_specs=[vmem, vmem, smem, vmem, vmem, vmem, vmem, smem, smem, smem],
        out_specs=(vmem, vmem, vmem),
        scratch_shapes=[
            pltpu.VMEM((SLOTS, 12, N), f32),
            pltpu.VMEM((SLOTS, 24, N), f32),
            pltpu.VMEM((SLOTS, 24, N), f32),
            pltpu.VMEM((SLOTS, 12, N), f32),
            pltpu.VMEM((SLOTS, 12, N), f32),
            pltpu.VMEM((STEPS, SLOTS, 12, N), f32),
            pltpu.VMEM((STEPS, SLOTS, 12, N), f32),
            pltpu.VMEM((PAIRS, N, N), bf16),
            pltpu.VMEM((6, N, N), bf16),
            pltpu.VMEM((OWN, 48, N), bf16),
            pltpu.VMEM((OWN, 48, N), bf16),
            pltpu.VMEM((OWN, 16, N), f32),
            pltpu.VMEM((16, N), f32),
            pltpu.VMEM((16, N), f32),
            pltpu.VMEM((16, N), f32),
            pltpu.VMEM((16, N), f32),
            pltpu.VMEM((16, N), f32),
            pltpu.VMEM((3 * PAIRS, N), f32),
            pltpu.VMEM((SLOTS * 16, 128), bf16),
            pltpu.VMEM((N, N), bf16),
            pltpu.VMEM((N, N), bf16),
            dma((5, 11)),
            dma((5, SLOTS)),
            dma((STEPS, 11)),
            dma((STEPS, SLOTS)),
        ],
        compiler_params=pltpu.CompilerParams(collective_id=0, has_side_effects=True),
        name="red_cell_steps",
    )(
        turn(positions),
        turn(rest_shape),
        modulus,
        stiffness,
        turn(wall_points),
        turn(density),
        wall_operator,
        seg_count,
        neighbours,
        near_patches.T,
    )
    return tuple(turn(out) for out in outs)


def solution(mesh):
    placed = (
        P(("seg", "cell"), None, None),
        P(("seg", "cell"), None, None),
        P(("seg", "cell")),
        P(),
        P(("seg", "cell"), None, None),
        P(("seg", "cell"), None, None),
        P(),
        P("seg"),
        P(("seg", "cell"), None),
        P(("seg", "cell"), None),
    )
    return jax.shard_map(
        body,
        mesh=mesh,
        in_specs=placed,
        out_specs=(
            P(("seg", "cell"), None, None),
            P(("seg", "cell"), None, None),
            P(("seg", "cell"), None, None),
        ),
        check_vma=False,
    )
```

time: 60.7 us -> 50.4 us (0.83)
  the two profiles are of different devices: /device:TPU:31 before, /device:TPU:1 now
where the time goes in v1:
time: 50.4 us; the launch traced here: 50.1 us
  Pallas kernels  46.1 us (91%)
  local copies, waits for them, and re-layouts  2.71 us (5%)
  between operations  1.3 us (3%)
    pallas_call x1, Pallas kernels, body(): pl.pallas_call(functools.partial(fused, nseg), out_shape=(shape, shape, s...  46.1 us
    unnamed x7, local copies, waits for them, and re-layouts  2.71 us

profile of v1, /device:TPU:1, one launch (start us, length us, event | category | flops | bytes accessed | tf_op | source)
XLA Modules:
  0.0 50.1 jit_solution(11428848599497395875)
XLA Ops:
  1.3 46.1 %red_cell_steps.1 = (f32[3,4,512]{2,1,0:T(4,128)}, f32[3,4,512]{2,1,0:T(4,128)}, f32[3,4,512]{2,1,0:T(4,128)}) custom-call(f32[3,4,512]{2,1,0:T(4,128)} %bitcast.11, f32[3,4,512]{2,1,0:T(4,128)} %bitcast.12, f32[4]{0:T(128)} %modulus.1, bf16[512,512]{1,0:T(8,128)(2,1)} %stiffness.1, f32[3,4,512]{2,1,0:T(4,128)} %bitcast.13, f32[3,4,512]{2,1,0:T(4,128)} %bitcast.14, ...), custom_call_target="tpu_custom_call" | custom-call | tf_op jit(solution)/shard_map/red_cell_steps/pallas_call | solution.py:454
  47.4 0.0 copy-start.1
  47.4 1.4 %copy.17 = f32[4,3,512]{2,0,1:T(4,128)} copy(f32[4,3,512]{2,0,1:T(4,128)} %bitcast.10) | data formatting | bytes 49152
  48.7 0.0 copy-done.1
  48.7 0.0 copy-start
  48.7 0.6 %copy.18 = f32[4,3,512]{2,0,1:T(4,128)} copy(f32[4,3,512]{2,0,1:T(4,128)S(1)} %bitcast.9) | data formatting | bytes 49152
  49.3 0.1 copy-done
  49.5 0.6 %copy.19 = f32[4,3,512]{2,0,1:T(4,128)} copy(f32[4,3,512]{2,0,1:T(4,128)S(1)} %bitcast.8) | data formatting | bytes 49152
Async XLA Ops:
  47.4 1.4 %copy-start.1 = (f32[3,4,512]{2,1,0:T(4,128)S(1)}, f32[3,4,512]{2,1,0:T(4,128)}, u32[]{:S(2)}) copy-start(f32[3,4,512]{2,1,0:T(4,128)} %get-tuple-element.7) | copy-start | bytes 73732
  48.7 0.7 %copy-start = (f32[3,4,512]{2,1,0:T(4,128)S(1)}, f32[3,4,512]{2,1,0:T(4,128)}, u32[]{:S(2)}) copy-start(f32[3,4,512]{2,1,0:T(4,128)} %get-tuple-element.8) | copy-start | bytes 73732

commit v2 on v1

--- a/solution.py
+++ b/solution.py
@@ -88,7 +88,7 @@
 
 
 def kernel_tile(squares):
-    inverse = lax.rsqrt(jnp.maximum(squares, soften_square))
+    inverse = lax.rsqrt(squares)
     return (inverse * inverse * inverse).astype(bf16)
 
 
@@ -248,8 +248,8 @@
         buffer[own, 12:24, :] = force[0:12, :]
         den_messages[step].buffer[own] = den[0:12, :]
 
-    def itself():
-        for c in range(OWN):
+    def itself(cells):
+        for c in cells:
             x, f = rows_of(pos, c), rows_of(force, c)
             g, b = moments(x, f), target_factor(x)
             gcell[c] = g
@@ -378,37 +378,43 @@
             hit = fits & (row_item + g * OWN == wanted)
             onehot[pl.ds(g * 16, 16), :] = jnp.where(hit, 1.0, 0.0).astype(bf16)
 
+    pl.semaphore_wait(barrier, len(peers))
+    walls.start()
     make_forces()
     pack(0)
+    cell_messages[0].start()
+    itself((0, 1))
+    walls.relay(1, 3)
+    itself((2, 3))
+    walls.relay(2)
+    den_messages[0].start()
     choose()
+    cell_messages[0].relay(1, 3)
     lax.fori_loop(0, N // 64, cut, 0)
-
-    pl.semaphore_wait(barrier, len(peers))
-    walls.start()
-    cell_messages[0].start()
-    itself()
-    walls.relay(1, 3, 2)
-    den_messages[0].start()
+    cell_messages[0].relay(2)
     walls.arrived()
-    cell_messages[0].relay(1, 3)
 
     for step in range(STEPS):
         cells, dens = cell_messages[step], den_messages[step]
-        if step == 1:
+        if step == 0:
+            by_halves(reverse, lambda: dens.relay(1, 3))
+            dens.relay(2)
+        else:
             make_forces()
             pack(step)
             cells.start()
             dens.start()
-            itself()
-            by_halves(reverse, lambda: cells.relay(1, 3))
-        else:
-            by_halves(reverse, lambda: cells.relay(2))
-        if step == 1:
-            cells.relay(2)
+            itself((0, 1, 2, 3))
+            cells.relay(1, 3)
+
+            def between():
+                cells.relay(2)
+                dens.relay(1, 3)
+
+            by_halves(reverse, between)
+            dens.relay(2)
         send_pieces(step)
-        dens.relay(1, 3)
         layered = operate()
-        dens.relay(2)
         cells.arrived()
         by_halves(functools.partial(listed, step), lambda: None)
         dens.arrived()

time: 50.4 us -> 47.7 us (0.946)
  Pallas kernels: 46.1 us -> 43.4 us
    pallas_call x1, Pallas kernels: 46.1 us -> 43.4 us  [body(): pl.pallas_call(functools.partial(fused, nseg), out_shape=(shape, shape, s...]
where the time goes in v2:
time: 47.7 us; the launch traced here: 47.4 us
  Pallas kernels  43.4 us (91%)
  local copies, waits for them, and re-layouts  2.71 us (6%)
  between operations  1.3 us (3%)
    pallas_call x1, Pallas kernels, body(): pl.pallas_call(functools.partial(fused, nseg), out_shape=(shape, shape, s...  43.4 us
    unnamed x7, local copies, waits for them, and re-layouts  2.71 us

profile of v2, /device:TPU:1, one launch (start us, length us, event | category | flops | bytes accessed | tf_op | source)
XLA Modules:
  0.0 47.4 jit_solution(13525086106805201948)
XLA Ops:
  1.3 43.4 %red_cell_steps.1 = (f32[3,4,512]{2,1,0:T(4,128)}, f32[3,4,512]{2,1,0:T(4,128)}, f32[3,4,512]{2,1,0:T(4,128)}) custom-call(f32[3,4,512]{2,1,0:T(4,128)} %bitcast.11, f32[3,4,512]{2,1,0:T(4,128)} %bitcast.12, f32[4]{0:T(128)} %modulus.1, bf16[512,512]{1,0:T(8,128)(2,1)} %stiffness.1, f32[3,4,512]{2,1,0:T(4,128)} %bitcast.13, f32[3,4,512]{2,1,0:T(4,128)} %bitcast.14, ...), custom_call_target="tpu_custom_call" | custom-call | tf_op jit(solution)/shard_map/red_cell_steps/pallas_call | solution.py:460
  44.7 0.0 copy-start.1
  44.7 1.4 %copy.17 = f32[4,3,512]{2,0,1:T(4,128)} copy(f32[4,3,512]{2,0,1:T(4,128)} %bitcast.10) | data formatting | bytes 49152
  46.1 0.0 copy-done.1
  46.1 0.0 copy-start
  46.1 0.6 %copy.18 = f32[4,3,512]{2,0,1:T(4,128)} copy(f32[4,3,512]{2,0,1:T(4,128)S(1)} %bitcast.9) | data formatting | bytes 49152
  46.7 0.1 copy-done
  46.8 0.6 %copy.19 = f32[4,3,512]{2,0,1:T(4,128)} copy(f32[4,3,512]{2,0,1:T(4,128)S(1)} %bitcast.8) | data formatting | bytes 49152
Async XLA Ops:
  44.7 1.4 %copy-start.1 = (f32[3,4,512]{2,1,0:T(4,128)S(1)}, f32[3,4,512]{2,1,0:T(4,128)}, u32[]{:S(2)}) copy-start(f32[3,4,512]{2,1,0:T(4,128)} %get-tuple-element.7) | copy-start | bytes 73732
  46.1 0.7 %copy-start = (f32[3,4,512]{2,1,0:T(4,128)S(1)}, f32[3,4,512]{2,1,0:T(4,128)}, u32[]{:S(2)}) copy-start(f32[3,4,512]{2,1,0:T(4,128)} %get-tuple-element.8) | copy-start | bytes 73732

commit v3 on v2

--- a/solution.py
+++ b/solution.py
@@ -145,23 +145,33 @@
     z = lax.axis_index("cell")
     odd = seg % 2
     partner = seg + 1 - 2 * odd
-    across = (seg + 2 * odd - 1 + nseg) % nseg
     own = NZ + z
 
     def turned(d):
         return (z + d) % NZ
 
-    peers = []
-    for away in (0, 1, -1):
-        for d in range(NZ):
-            if away or d:
-                peers.append((away, d))
+    beside = seg + 2 * odd - 1
+    inside = (beside >= 0) & (beside < nseg)
+    across = (beside + nseg) % nseg
+    toward = 1 - 2 * odd
+
+    same = [(seg, 0, d) for d in (1, 2, 3)]
+    near_peers = same + [(partner, toward, d) for d in range(NZ)]
+    far_peers = [(across, -toward, d) for d in range(NZ)]
 
     barrier = pltpu.get_barrier_semaphore()
-    for away, d in peers:
-        pl.semaphore_signal(
-            barrier, inc=1, device_id=((seg + away + nseg) % nseg, turned(d)), device_id_type=MESH
-        )
+
+    def greet(peers):
+        for segment, _, d in peers:
+            pl.semaphore_signal(
+                barrier, inc=1, device_id=(segment, turned(d)), device_id_type=MESH
+            )
+
+    @pl.when(inside)
+    def _():
+        greet(far_peers)
+
+    greet(near_peers)
 
     for ref in (pos, rest, force, den, vel):
         ref[...] = jnp.zeros_like(ref)
@@ -197,25 +207,45 @@
         def start(self):
             for k, d in enumerate((1, 3, 2)):
                 self.copy(own, own, (seg, turned(d)), k).start()
-            self.copy(own, 8 - 8 * odd + z, (across, z), 4).start()
+
+            @pl.when(inside)
+            def _():
+                self.copy(own, 8 - 8 * odd + z, (across, z), 4).start()
+
             self.copy(own, 8 * odd + z, (partner, z), 3).start()
 
         def relay(self, *which):
             for d in which:
                 slot = NZ + turned(d)
                 self.copy(slot, slot, (seg, turned(d)), 0).wait_recv()
+                self.hand_on(slot, d)
+
+        def hand_on(self, slot, d):
+            @pl.when(inside)
+            def _():
                 self.copy(slot, 8 - 8 * odd + turned(d), (across, z), 3 + 2 * d).start()
-                self.copy(slot, 8 * odd + turned(d), (partner, z), 4 + 2 * d).start()
+
+            self.copy(slot, 8 * odd + turned(d), (partner, z), 4 + 2 * d).start()
 
         def arrived(self):
             for d in range(NZ):
-                for base in (0, 8):
-                    slot = base + turned(d)
+                slot = 8 - 8 * odd + turned(d)
+                self.copy(slot, slot, (partner, z), 0).wait_recv()
+
+            @pl.when(inside)
+            def _():
+                for d in range(NZ):
+                    slot = 8 * odd + turned(d)
                     self.copy(slot, slot, (partner, z), 0).wait_recv()
 
         def sent(self):
-            for k in range(11):
+            for k in (0, 1, 2, 3, 6, 8, 10):
                 self.copy(own, own, (partner, z), k).wait_send()
+
+            @pl.when(inside)
+            def _():
+                for k in (4, 5, 7, 9):
+                    self.copy(own, own, (partner, z), k).wait_send()
 
     walls = Message(wall, 0)
     cell_messages = [Message(cells_first, 1), Message(cells_second, 2)]
@@ -242,11 +272,16 @@
         offset = (pos[...] - rest[...]).astype(bf16)
         force[...] = mt(offset, stiffness[...]) * scale
 
-    def pack(step):
+    def send_cells(step):
+        make_forces()
         buffer = cell_messages[step].buffer
         buffer[own, 0:12, :] = pos[0:12, :]
         buffer[own, 12:24, :] = force[0:12, :]
+        cell_messages[step].start()
+
+    def send_density(step):
         den_messages[step].buffer[own] = den[0:12, :]
+        den_messages[step].start()
 
     def itself(cells):
         for c in cells:
@@ -325,13 +360,20 @@
         shares = mm(onehot[...], spread)
         for g in range(SLOTS):
             xsend[step, g] = shares[g * 16 : g * 16 + 12]
-        for k, (away, d) in enumerate(peers):
+        @pl.when(inside)
+        def _():
+            start_shares(step, far_peers, 7)
+
+        start_shares(step, near_peers, 0)
+
+    def start_shares(step, peers, base):
+        for k, (segment, away, d) in enumerate(peers):
             x_copy(
                 step,
                 (away + 1) * NZ + turned(d),
                 (1 - away) * NZ + z,
-                ((seg + away + nseg) % nseg, turned(d)),
-                k,
+                (segment, turned(d)),
+                base + k,
             ).start()
 
     def operate():
@@ -346,13 +388,21 @@
         pos[...] = pos[...] + time_step * speed
 
     def update_density(step, layered):
-        flow = xsend[step, own]
-        for k, (away, d) in enumerate(peers):
-            slot = (1 + away) * NZ + turned(d)
-            x_copy(step, own, slot, (seg, turned(d)), k).wait_recv()
-            flow = flow + xrecv[step, slot]
+        def taken(peers, flow):
+            for _, away, d in peers:
+                slot = (1 + away) * NZ + turned(d)
+                x_copy(step, own, slot, (partner, z), 0).wait_recv()
+                part = xrecv[step, slot]
+                flow = part if flow is None else flow + part
+            return flow
+
+        flow = taken(near_peers, xsend[step, own])
         old = den[0:12, :]
         den[0:12, :] = old - relax_factor * (flow + 0.5 * old + layered[0:12])
+
+        @pl.when(inside)
+        def _():
+            den[0:12, :] = den[0:12, :] - relax_factor * taken(far_peers, None)
 
     def cut(i, _):
         at = pl.ds(pl.multiple_of(i * 64, 64), 64)
@@ -378,20 +428,21 @@
             hit = fits & (row_item + g * OWN == wanted)
             onehot[pl.ds(g * 16, 16), :] = jnp.where(hit, 1.0, 0.0).astype(bf16)
 
-    pl.semaphore_wait(barrier, len(peers))
+    pl.semaphore_wait(
+        barrier, jnp.where(inside, len(near_peers) + len(far_peers), len(near_peers))
+    )
     walls.start()
-    make_forces()
-    pack(0)
-    cell_messages[0].start()
+    send_cells(0)
     itself((0, 1))
     walls.relay(1, 3)
     itself((2, 3))
     walls.relay(2)
-    den_messages[0].start()
+    send_density(0)
     choose()
     cell_messages[0].relay(1, 3)
     lax.fori_loop(0, N // 64, cut, 0)
     cell_messages[0].relay(2)
+    layered = operate()
     walls.arrived()
 
     for step in range(STEPS):
@@ -399,11 +450,8 @@
         if step == 0:
             by_halves(reverse, lambda: dens.relay(1, 3))
             dens.relay(2)
+            send_pieces(step)
         else:
-            make_forces()
-            pack(step)
-            cells.start()
-            dens.start()
             itself((0, 1, 2, 3))
             cells.relay(1, 3)
 
@@ -413,21 +461,30 @@
 
             by_halves(reverse, between)
             dens.relay(2)
-        send_pieces(step)
-        layered = operate()
+            send_pieces(step)
+            layered = operate()
         cells.arrived()
         by_halves(functools.partial(listed, step), lambda: None)
         dens.arrived()
         by_halves(functools.partial(from_walls, step), lambda: None)
         move()
+        if step + 1 < STEPS:
+            send_cells(step + 1)
         update_density(step, layered)
+        if step + 1 < STEPS:
+            send_density(step + 1)
 
     walls.sent()
     for step in range(STEPS):
         cell_messages[step].sent()
         den_messages[step].sent()
-        for k in range(11):
+        for k in range(7):
             x_copy(step, own, own, (partner, z), k).wait_send()
+
+        @pl.when(inside)
+        def _():
+            for k in range(7, 11):
+                x_copy(step, own, own, (partner, z), k).wait_send()
 
     for k in range(3):
         at = pl.ds(4 * k, 4)

time: 47.7 us -> 44.6 us (0.935)
  the two profiles are of different devices: /device:TPU:1 before, /device:TPU:6 now
where the time goes in v3:
time: 44.6 us; the launch traced here: 44.3 us
  Pallas kernels  40.3 us (90%)
  local copies, waits for them, and re-layouts  2.71 us (6%)
  between operations  1.3 us (3%)
    pallas_call x1, Pallas kernels, body(): pl.pallas_call(functools.partial(fused, nseg), out_shape=(shape, shape, s...  40.3 us
    unnamed x7, local copies, waits for them, and re-layouts  2.71 us

profile of v3, /device:TPU:6, one launch (start us, length us, event | category | flops | bytes accessed | tf_op | source)
XLA Modules:
  0.0 44.3 jit_solution(3757897387171583364)
XLA Ops:
  1.3 40.3 %red_cell_steps.1 = (f32[3,4,512]{2,1,0:T(4,128)}, f32[3,4,512]{2,1,0:T(4,128)}, f32[3,4,512]{2,1,0:T(4,128)}) custom-call(f32[3,4,512]{2,1,0:T(4,128)} %bitcast.11, f32[3,4,512]{2,1,0:T(4,128)} %bitcast.12, f32[4]{0:T(128)} %modulus.1, bf16[512,512]{1,0:T(8,128)(2,1)} %stiffness.1, f32[3,4,512]{2,1,0:T(4,128)} %bitcast.13, f32[3,4,512]{2,1,0:T(4,128)} %bitcast.14, ...), custom_call_target="tpu_custom_call" | custom-call | tf_op jit(solution)/shard_map/red_cell_steps/pallas_call | solution.py:517
  41.6 0.0 copy-start.1
  41.6 1.4 %copy.17 = f32[4,3,512]{2,0,1:T(4,128)} copy(f32[4,3,512]{2,0,1:T(4,128)} %bitcast.10) | data formatting | bytes 49152
  42.9 0.0 copy-done.1
  42.9 0.0 copy-start
  42.9 0.6 %copy.18 = f32[4,3,512]{2,0,1:T(4,128)} copy(f32[4,3,512]{2,0,1:T(4,128)S(1)} %bitcast.9) | data formatting | bytes 49152
  43.5 0.1 copy-done
  43.7 0.6 %copy.19 = f32[4,3,512]{2,0,1:T(4,128)} copy(f32[4,3,512]{2,0,1:T(4,128)S(1)} %bitcast.8) | data formatting | bytes 49152
Async XLA Ops:
  41.6 1.4 %copy-start.1 = (f32[3,4,512]{2,1,0:T(4,128)S(1)}, f32[3,4,512]{2,1,0:T(4,128)}, u32[]{:S(2)}) copy-start(f32[3,4,512]{2,1,0:T(4,128)} %get-tuple-element.7) | copy-start | bytes 73732
  42.9 0.7 %copy-start = (f32[3,4,512]{2,1,0:T(4,128)S(1)}, f32[3,4,512]{2,1,0:T(4,128)}, u32[]{:S(2)}) copy-start(f32[3,4,512]{2,1,0:T(4,128)} %get-tuple-element.8) | copy-start | bytes 73732

commit v4 on v3

--- a/solution.py
+++ b/solution.py
@@ -105,16 +105,14 @@
     pos_in,
     rest_in,
     modulus,
-    stiffness,
+    stiffness_in,
     points_in,
     density_in,
-    operator,
+    operator_in,
     seg_count,
     neighbours,
     near,
-    pos_out,
-    vel_out,
-    den_out,
+    out,
     wall,
     cells_first,
     cells_second,
@@ -140,7 +138,14 @@
     recv_sem,
     x_send,
     x_recv,
+    stiffness,
+    operator,
+    load_sem,
 ):
+    load_stiffness = pltpu.make_async_copy(stiffness_in, stiffness, load_sem.at[0])
+    load_operator = pltpu.make_async_copy(operator_in, operator, load_sem.at[1])
+    load_stiffness.start()
+    load_operator.start()
     seg = lax.axis_index("seg")
     z = lax.axis_index("cell")
     odd = seg % 2
@@ -432,6 +437,7 @@
         barrier, jnp.where(inside, len(near_peers) + len(far_peers), len(near_peers))
     )
     walls.start()
+    load_stiffness.wait()
     send_cells(0)
     itself((0, 1))
     walls.relay(1, 3)
@@ -440,6 +446,7 @@
     send_density(0)
     choose()
     cell_messages[0].relay(1, 3)
+    load_operator.wait()
     lax.fori_loop(0, N // 64, cut, 0)
     cell_messages[0].relay(2)
     layered = operate()
@@ -454,15 +461,11 @@
         else:
             itself((0, 1, 2, 3))
             cells.relay(1, 3)
-
-            def between():
-                cells.relay(2)
-                dens.relay(1, 3)
-
-            by_halves(reverse, between)
+            layered = operate()
+            cells.relay(2)
+            by_halves(reverse, lambda: dens.relay(1, 3))
             dens.relay(2)
             send_pieces(step)
-            layered = operate()
         cells.arrived()
         by_halves(functools.partial(listed, step), lambda: None)
         dens.arrived()
@@ -488,9 +491,14 @@
 
     for k in range(3):
         at = pl.ds(4 * k, 4)
-        pos_out[k] = pos[at, :]
-        vel_out[k] = vel[at, :]
-        den_out[k] = den[at, :]
+        out[0, k] = pos[at, :]
+        out[1, k] = vel[at, :]
+        out[2, k] = den[at, :]
+
+
+def part_results(state, pos_out, vel_out, den_out):
+    for k, ref in enumerate((pos_out, vel_out, den_out)):
+        ref[...] = state[k]
 
 
 def body(
@@ -508,17 +516,18 @@
     nseg = lax.axis_size("seg")
     vmem = pl.BlockSpec(memory_space=pltpu.VMEM)
     smem = pl.BlockSpec(memory_space=pltpu.SMEM)
+    hbm = pl.BlockSpec(memory_space=pl.ANY)
     shape = jax.ShapeDtypeStruct((3, OWN, N), f32)
     dma = pltpu.SemaphoreType.DMA
 
     def turn(array):
         return jnp.transpose(array, (1, 0, 2))
 
-    outs = pl.pallas_call(
+    state = pl.pallas_call(
         functools.partial(fused, nseg),
-        out_shape=(shape, shape, shape),
-        in_specs=[vmem, vmem, smem, vmem, vmem, vmem, vmem, smem, smem, smem],
-        out_specs=(vmem, vmem, vmem),
+        out_shape=jax.ShapeDtypeStruct((3, 3, OWN, N), f32),
+        in_specs=[vmem, vmem, smem, hbm, vmem, vmem, hbm, smem, smem, smem],
+        out_specs=vmem,
         scratch_shapes=[
             pltpu.VMEM((SLOTS, 12, N), f32),
             pltpu.VMEM((SLOTS, 24, N), f32),
@@ -545,6 +554,9 @@
             dma((5, SLOTS)),
             dma((STEPS, 11)),
             dma((STEPS, SLOTS)),
+            pltpu.VMEM((N, N), bf16),
+            pltpu.VMEM((N, N), f32),
+            dma((2,)),
         ],
         compiler_params=pltpu.CompilerParams(collective_id=0, has_side_effects=True),
         name="red_cell_steps",
@@ -560,6 +572,13 @@
         neighbours,
         near_patches.T,
     )
+    outs = pl.pallas_call(
+        part_results,
+        out_shape=(shape, shape, shape),
+        in_specs=[vmem],
+        out_specs=(vmem, vmem, vmem),
+        name="part_results",
+    )(state)
     return tuple(turn(out) for out in outs)
 
 

time: 44.6 us -> 41.8 us (0.937)
  local copies, waits for them, and re-layouts: 2.71 us -> 0 us
    unnamed x7 -> x0, local copies, waits for them, and re-layouts: 2.71 us -> none
    pallas_call x1 -> x2, Pallas kernels: 40.3 us -> 40.2 us  [the longest x1 38.7 us: body(): pl.pallas_call(functools.partial(fused, nseg), out_shape=jax.ShapeDtypeSt...]
where the time goes in v4:
time: 41.8 us; the launch traced here: 41.5 us
  Pallas kernels  40.2 us (96%)
  between operations  1.29 us (3%)
    pallas_call x1, Pallas kernels, body(): pl.pallas_call(functools.partial(fused, nseg), out_shape=jax.ShapeDtypeSt...  38.7 us
    pallas_call x1, Pallas kernels, body(): pl.pallas_call(part_results, out_shape=(shape, shape, shape), in_specs=[v...  1.51 us

profile of v4, /device:TPU:6, one launch (start us, length us, event | category | flops | bytes accessed | tf_op | source)
XLA Modules:
  0.0 41.5 jit_solution(14952466024003485238)
XLA Ops:
  1.3 38.7 %red_cell_steps.1.state = f32[3,3,4,512]{3,2,1,0:T(4,128)} custom-call(f32[3,4,512]{2,1,0:T(4,128)} %bitcast.8, f32[3,4,512]{2,1,0:T(4,128)} %bitcast.9, f32[4]{0:T(128)} %modulus.1, bf16[512,512]{1,0:T(8,128)(2,1)} %stiffness_in.1, f32[3,4,512]{2,1,0:T(4,128)} %bitcast.10, f32[3,4,512]{2,1,0:T(4,128)} %bitcast.11, f32[512,512]{1,0:T(8,128)} %operator_in.1, ...), custom_call_target="tpu_custom_call" | custom-call | tf_op jit(solution)/shard_map/red_cell_steps/pallas_call | solution.py:526
  40.0 1.5 %part_results.1 = (f32[3,4,512]{2,1,0:T(4,128)}, f32[3,4,512]{2,1,0:T(4,128)}, f32[3,4,512]{2,1,0:T(4,128)}) custom-call(f32[3,3,4,512]{3,2,1,0:T(4,128)} %red_cell_steps.1.state), custom_call_target="tpu_custom_call" | custom-call | tf_op jit(solution)/shard_map/part_results/pallas_call | solution.py:575

commit v5 on v4

--- a/solution.py
+++ b/solution.py
@@ -33,11 +33,8 @@
 
 
 def rows8(rows):
-    index = lax.broadcasted_iota(jnp.int32, (8, N), 0)
-    out = jnp.zeros((8, N), f32)
-    for k, row in enumerate(rows):
-        out = jnp.where(index == k, jnp.broadcast_to(row, (8, N)), out)
-    return out
+    rows = list(rows) + [jnp.zeros_like(rows[0])] * (8 - len(rows))
+    return jnp.concatenate(rows, 0)
 
 
 def dot3(a, b):
@@ -298,16 +295,9 @@
             acc[c] = fold(mm(g, pbuf[c]))
 
     def by_halves(work, between):
-        def trip(h, _):
-            work(2 * h)
-
-            @pl.when(h == 0)
-            def _():
-                between()
-
-            return 0
-
-        lax.fori_loop(0, 2, trip, 0)
+        work(0)
+        between()
+        work(2)
 
     def reverse(cell):
         for i in range(2):

time: 41.8 us -> 41 us (0.981); the launches traced: 41.5 us -> 40.1 us
  Pallas kernels: 40.2 us -> 38.9 us
    pallas_call x1, Pallas kernels: 38.7 us -> 37.3 us  [body(): pl.pallas_call(functools.partial(fused, nseg), out_shape=jax.ShapeDtypeSt...]
where the time goes in v5:
time: 41 us; the launch traced here: 40.1 us
  Pallas kernels  38.9 us (95%)
  between operations  1.29 us (3%)
    pallas_call x1, Pallas kernels, body(): pl.pallas_call(functools.partial(fused, nseg), out_shape=jax.ShapeDtypeSt...  37.3 us
    pallas_call x1, Pallas kernels, body(): pl.pallas_call(part_results, out_shape=(shape, shape, shape), in_specs=[v...  1.51 us

profile of v5, /device:TPU:6, one launch (start us, length us, event | category | flops | bytes accessed | tf_op | source)
XLA Modules:
  0.0 40.1 jit_solution(4521002205494185)
XLA Ops:
  1.3 37.3 %red_cell_steps.1.state = f32[3,3,4,512]{3,2,1,0:T(4,128)} custom-call(f32[3,4,512]{2,1,0:T(4,128)} %bitcast.8, f32[3,4,512]{2,1,0:T(4,128)} %bitcast.9, f32[4]{0:T(128)} %modulus.1, bf16[512,512]{1,0:T(8,128)(2,1)} %stiffness_in.1, f32[3,4,512]{2,1,0:T(4,128)} %bitcast.10, f32[3,4,512]{2,1,0:T(4,128)} %bitcast.11, f32[512,512]{1,0:T(8,128)} %operator_in.1, ...), custom_call_target="tpu_custom_call" | custom-call | tf_op jit(solution)/shard_map/red_cell_steps/pallas_call | solution.py:516
  38.6 1.5 %part_results.1 = (f32[3,4,512]{2,1,0:T(4,128)}, f32[3,4,512]{2,1,0:T(4,128)}, f32[3,4,512]{2,1,0:T(4,128)}) custom-call(f32[3,3,4,512]{3,2,1,0:T(4,128)} %red_cell_steps.1.state), custom_call_target="tpu_custom_call" | custom-call | tf_op jit(solution)/shard_map/part_results/pallas_call | solution.py:565

commit v6 on v5

--- a/solution.py
+++ b/solution.py
@@ -57,12 +57,13 @@
     p, g = dot3(y, y), dot3(y, f)
     one = rows8([f[0], f[1], f[2], g] + [p * f[k] + g * y[k] for k in range(3)] + [f[0] * y[0]])
     two = rows8([f[l] * y[k] for l in range(3) for k in range(3)][1:])
-    a, b, c = split3(jnp.concatenate([one, two], 0))
-    return jnp.concatenate([a, b, c], 0).astype(bf16)
+    a, b, _ = split3(jnp.concatenate([one, two], 0))
+    return jnp.concatenate([a, b], 0).astype(bf16)
 
 
 def fold(sums):
-    return sums[0:16] + sums[16:32] + sums[32:48]
+    total = sums[0:16] + sums[16:32]
+    return total + sums[32:48] if sums.shape[0] == 48 else total
 
 
 def combine(sums, x):
@@ -528,7 +529,7 @@
             pltpu.VMEM((STEPS, SLOTS, 12, N), f32),
             pltpu.VMEM((PAIRS, N, N), bf16),
             pltpu.VMEM((6, N, N), bf16),
-            pltpu.VMEM((OWN, 48, N), bf16),
+            pltpu.VMEM((OWN, 32, N), bf16),
             pltpu.VMEM((OWN, 48, N), bf16),
             pltpu.VMEM((OWN, 16, N), f32),
             pltpu.VMEM((16, N), f32),

time: 41 us -> 40.9 us (level)
  no operation moved by 1% of the time
where the time goes in v6:
time: 40.9 us; the launch traced here: 40.1 us
  Pallas kernels  38.8 us (95%)
  between operations  1.29 us (3%)
    pallas_call x1, Pallas kernels, body(): pl.pallas_call(functools.partial(fused, nseg), out_shape=jax.ShapeDtypeSt...  37.3 us
    pallas_call x1, Pallas kernels, body(): pl.pallas_call(part_results, out_shape=(shape, shape, shape), in_specs=[v...  1.51 us

profile of v6, /device:TPU:6, one launch (start us, length us, event | category | flops | bytes accessed | tf_op | source)
XLA Modules:
  0.0 40.1 jit_solution(16914611239553925228)
XLA Ops:
  1.3 37.3 %red_cell_steps.1.state = f32[3,3,4,512]{3,2,1,0:T(4,128)} custom-call(f32[3,4,512]{2,1,0:T(4,128)} %bitcast.8, f32[3,4,512]{2,1,0:T(4,128)} %bitcast.9, f32[4]{0:T(128)} %modulus.1, bf16[512,512]{1,0:T(8,128)(2,1)} %stiffness_in.1, f32[3,4,512]{2,1,0:T(4,128)} %bitcast.10, f32[3,4,512]{2,1,0:T(4,128)} %bitcast.11, f32[512,512]{1,0:T(8,128)} %operator_in.1, ...), custom_call_target="tpu_custom_call" | custom-call | tf_op jit(solution)/shard_map/red_cell_steps/pallas_call | solution.py:517
  38.6 1.5 %part_results.1 = (f32[3,4,512]{2,1,0:T(4,128)}, f32[3,4,512]{2,1,0:T(4,128)}, f32[3,4,512]{2,1,0:T(4,128)}) custom-call(f32[3,3,4,512]{3,2,1,0:T(4,128)} %red_cell_steps.1.state), custom_call_target="tpu_custom_call" | custom-call | tf_op jit(solution)/shard_map/part_results/pallas_call | solution.py:566
